TPU v7x, 256 devices: a whole 4x4x8 slice. The times are simulated.
256 devices in a mesh: grp: 32 (over x, y, core), blk: 8 (over z).
Axes of the slice: x: 4, y: 4, z: 8, core: 2. Of those that a mesh axis runs over, the one named last changes fastest.
Arguments:
- tiles_near: bfloat16 [16384, 256, 256], P(('grp', 'blk')), may hold values from -0.078125 to 0.078125
- near_cols: int32 [256, 64], P(('grp', 'blk')), may hold values from 0 to 3
- tiles_far: bfloat16 [6144, 256, 256], P(('grp', 'blk')), may hold values from -0.078125 to 0.078125
- far_groups: int32 [256, 24], P(('grp', 'blk')), may hold values from 0 to 31, as said below
- need_blocks: int32 [256, 32], P(('grp', 'blk')), may hold values from -1 to 3, as said below
- start_vectors: bfloat16 [262144, 128], P(('grp', 'blk')), may hold values from -6 to 6
Outputs:
- vectors: float32 [262144, 128], P(('grp', 'blk'))
Inputs may be any that keep to these rules, and one draw needn't show every extreme that they name: need_blocks[d, h] is -1 for d's own group and for groups d reads nothing from, else a row block index below 4 of the device of group h at d's position along blk; every device reads from at least one other group. far_groups[d, t] is a group h with need_blocks[d, h] >= 0.
All inputs are finite; a program needn't handle non-finite values.
Results may differ from a plain program's by a relative error of at most 0.0029.
Values may be sent and summed in bfloat16 or wider, within the bound.
A program may use at most 128 MiB of HBM per device.

v0:
```python
import jax
import jax.numpy as jnp
from jax import lax
from jax.sharding import PartitionSpec as P

ITERS = 2


def per_device(tiles_near, near_cols, tiles_far, far_groups, need_blocks, start_vectors):
    tile_size = tiles_near.shape[1]
    vec_width = start_vectors.shape[1]
    blocks = start_vectors.shape[0] // tile_size
    group_size = lax.axis_size("blk")
    group_count = lax.axis_size("grp")
    per_source = tiles_near.shape[0] // (blocks * group_size)
    far_each = tiles_far.shape[0] // blocks
    near_tiles = tiles_near.reshape(blocks, group_size, per_source, tile_size, tile_size)
    near_index = near_cols.reshape(blocks, group_size, per_source)
    far_tiles = tiles_far.reshape(blocks, far_each, tile_size, tile_size)
    far_index = far_groups.reshape(blocks, far_each)
    wanted = need_blocks.reshape(group_count)
    total_rows = blocks * tile_size * group_size * group_count
    current = start_vectors
    vectors = start_vectors.astype(jnp.float32)
    for iteration in range(ITERS):
        local_rows = current.reshape(blocks, tile_size, vec_width)
        group_table = lax.all_gather(local_rows, "blk", axis=0, tiled=True)
        source_ids = jnp.arange(group_size, dtype=jnp.int32)[None, :, None]
        chosen = group_table[source_ids * blocks + near_index]
        near_part = jnp.einsum(
            "rmnij,rmnjk->rik", near_tiles, chosen, preferred_element_type=jnp.float32
        )
        everything = lax.all_gather(local_rows, "grp", axis=0, tiled=True)
        far_rows = everything[far_index * blocks + wanted[far_index]]
        far_part = jnp.einsum(
            "rnij,rnjk->rik", far_tiles, far_rows, preferred_element_type=jnp.float32
        )
        product = near_part + far_part
        flat_rows = product.reshape(blocks * tile_size, vec_width)
        local_gram = jnp.dot(
            flat_rows.T,
            flat_rows,
            precision=lax.Precision.HIGHEST,
            preferred_element_type=jnp.float32,
        )
        gram = lax.psum(local_gram, ("grp", "blk")) / total_rows
        factor = jnp.linalg.cholesky(gram)
        identity_matrix = jnp.eye(vec_width, dtype=jnp.float32)
        inverse = lax.linalg.triangular_solve(factor, identity_matrix, left_side=True, lower=True).T
        vectors = jnp.dot(
            flat_rows, inverse, precision=lax.Precision.HIGHEST, preferred_element_type=jnp.float32
        )
        current = vectors.astype(jnp.bfloat16)
    return vectors


def solution(mesh):
    in_specs = (
        P(("grp", "blk"), None, None),
        P(("grp", "blk"), None),
        P(("grp", "blk"), None, None),
        P(("grp", "blk"), None),
        P(("grp", "blk"), None),
        P(("grp", "blk"), None),
    )
    out_specs = P(("grp", "blk"), None)
    return jax.shard_map(
        per_device, mesh=mesh, in_specs=in_specs, out_specs=out_specs, check_vma=False
    )
```

profile of v0, /device:TPU:1, one launch (start us, length us, event | category | flops | bytes accessed | tf_op | source)
XLA Modules:
  0.0 777.3 jit_solution(7489281376360508679)
XLA Ops:
  6.5 0.7 all-gather.5.cloned.1.call-update
  7.3 0.7 all-gather.7.cloned.1.call-update
  8.1 0.5 broadcast.166
  8.6 1.3 reduce.10
  10.1 1.4 gather_fusion.1
  11.6 1.3 reduce.11
  12.9 0.1 reshape.117
  13.1 0.1 reshape.129
  13.3 37.1 %all-gather.5.cloned.1.call-done = bf16[32,256,128]{2,1,0:T(8,128)(2,1)} async-done(((bf16[4,256,128]{2,1,0:T(8,128)(2,1)}), bf16[32,256,128]{2,1,0:T(8,128)(2,1)}) %all-gather.5.cloned.1.call-update) | async-done | bytes 2097168 | tf_op jit(solution)/shard_map/all_gather | solution.py:27
  50.4 4.6 gather_fusion
  55.0 58.5 %all-gather.7.cloned.1.call-done = bf16[128,256,128]{2,1,0:T(8,128)(2,1)} async-done(((bf16[4,256,128]{2,1,0:T(8,128)(2,1)}), bf16[128,256,128]{2,1,0:T(8,128)(2,1)}) %all-gather.7.cloned.1.call-update) | async-done | bytes 8388624 | tf_op jit(solution)/shard_map/all_gather | solution.py:33
  113.6 5.4 gather_fusion.2
  118.9 2.7 convolution_bitcast_fusion.1
  121.7 5.2 fusion.31
  126.9 0.8 copy-done.1
  127.7 1.2 convolution_bitcast_fusion.3
  129.0 2.0 copy.32
  131.0 235.3 %all-reduce.3.cloned.1.call-done = f32[128,128]{0,1:T(8,128)} async-done(((f32[128,128]{0,1:T(8,128)}), f32[128,128]{0,1:T(8,128)}) %all-reduce.3.cloned.1.call-update) | async-done | bytes 65552 | tf_op jit(solution)/shard_map/psum | solution.py:46
  366.3 0.8 broadcast_multiply_fusion.1
  367.2 0.1 copy.35
  367.3 0.9 fusion.45
  368.1 11.7 %cholesky.44 = f32[128,128]{1,0:T(8,128)S(1)} custom-call(f32[128,128]{1,0:T(8,128)S(1)} %fusion.45), custom_call_target="Cholesky" | custom-call | tf_op jit(solution)/shard_map/jit(cholesky)/cholesky | solution.py:47
  379.9 0.6 compare_reduce_fusion.1
  380.5 0.7 fusion.40
  381.2 9.8 %custom-call.6 = f32[1,128,128]{1,2,0:T(8,128)S(1)} custom-call(f32[1,128,128]{2,1,0:T(8,128)S(1)} %fusion.40), custom_call_target="InvertDiagBlocksLowerTriangular" | custom-call | tf_op jit(solution)/shard_map/triangular_solve/custom-call.0 | solution.py:49
  391.0 0.3 fusion.38
  391.3 2.3 convolution_convert_fusion
  393.7 0.5 all-gather.11.cloned.1.call-update
  394.2 0.2 all-reduce.5.cloned.1.call-start
  394.5 32.8 %all-gather.9.cloned.1.call-done = bf16[32,256,128]{2,1,0:T(8,128)(2,1)} async-done(((bf16[4,256,128]{2,1,0:T(8,128)(2,1)}), bf16[32,256,128]{2,1,0:T(8,128)(2,1)}) %all-gather.9.cloned.1.call-update) | async-done | bytes 2097168 | tf_op jit(solution)/shard_map/all_gather | solution.py:27
  427.3 4.6 gather_fusion.3
  432.0 58.4 %all-gather.11.cloned.1.call-done = bf16[128,256,128]{2,1,0:T(8,128)(2,1)} async-done(((bf16[4,256,128]{2,1,0:T(8,128)(2,1)}), bf16[128,256,128]{2,1,0:T(8,128)(2,1)}) %all-gather.11.cloned.1.call-update) | async-done | bytes 8388624 | tf_op jit(solution)/shard_map/all_gather | solution.py:33
  490.3 5.4 gather_fusion.4
  495.7 2.7 convolution_bitcast_fusion
  498.4 5.2 fusion.21
  503.7 0.8 copy-done.2
  504.5 1.2 convolution_bitcast_fusion.2
  505.7 2.0 copy.39
  507.7 235.3 %all-reduce.5.cloned.1.call-done = f32[128,128]{0,1:T(8,128)} async-done(((f32[128,128]{0,1:T(8,128)}), f32[128,128]{0,1:T(8,128)}) %all-reduce.5.cloned.1.call-update) | async-done | bytes 65552 | tf_op jit(solution)/shard_map/psum | solution.py:46
  743.1 0.8 broadcast_multiply_fusion
  743.9 0.1 copy.42
  744.0 0.9 fusion.43
  744.9 11.7 %cholesky.55 = f32[128,128]{1,0:T(8,128)S(1)} custom-call(f32[128,128]{1,0:T(8,128)S(1)} %fusion.43), custom_call_target="Cholesky" | custom-call | tf_op jit(solution)/shard_map/jit(cholesky)/cholesky | solution.py:47
  756.6 0.6 compare_reduce_fusion
  757.2 0.7 fusion.41
  757.9 9.8 %custom-call.7 = f32[1,128,128]{1,2,0:T(8,128)S(1)} custom-call(f32[1,128,128]{2,1,0:T(8,128)S(1)} %fusion.41), custom_call_target="InvertDiagBlocksLowerTriangular" | custom-call | tf_op jit(solution)/shard_map/triangular_solve/custom-call.0 | solution.py:49
  767.7 0.3 fusion.36
  768.0 2.4 fusion.46
  (29 shorter events, 0.8 us)
Async XLA Ops:
  6.5 112.4 %copy-start = (bf16[24,256,256]{2,1,0:T(8,128)(2,1)S(1)}, bf16[24,256,256]{2,1,0:T(8,128)(2,1)}, u32[]{:S(2)}) copy-start(bf16[24,256,256]{2,1,0:T(8,128)(2,1)} %param.11) | copy-start | bytes 9437188
  6.5 43.8 %all-gather.5.cloned.1.call-start = ((), (), s32[]{:S(2)}) async-start(), calls=%async_computation | async-start | bytes 2359296 | tf_op jit(solution)/shard_map/all_gather | solution.py:27
  7.3 106.3 %all-gather.7.cloned.1.call-start = ((), (), s32[]{:S(2)}) async-start(), calls=%async_computation.1 | async-start | bytes 8650752 | tf_op jit(solution)/shard_map/all_gather | solution.py:33
  8.0 358.3 %all-reduce.3.cloned.1.call-start = ((), (), s32[]{:S(2)}) async-start(), calls=%async_computation.2 | async-start | bytes 131072 | tf_op jit(solution)/shard_map/psum | solution.py:46
  118.9 2.7 copy-start.4
  126.9 0.8 copy-start.1
  128.9 298.4 %all-gather.9.cloned.1.call-start = ((), (), s32[]{:S(2)}) async-start(), calls=%async_computation.3 | async-start | bytes 2359296 | tf_op jit(solution)/shard_map/all_gather | solution.py:27
  393.6 96.7 %all-gather.11.cloned.1.call-start = ((), (), s32[]{:S(2)}) async-start(), calls=%async_computation.4 | async-start | bytes 8650752 | tf_op jit(solution)/shard_map/all_gather | solution.py:33
  394.2 348.8 %all-reduce.5.cloned.1.call-start = ((), (), s32[]{:S(2)}) async-start(), calls=%async_computation.5 | async-start | bytes 131072 | tf_op jit(solution)/shard_map/psum | solution.py:46
  495.7 2.7 copy-start.3
  503.7 0.8 copy-start.2
Sparse Core Ops, SparseCore 0:
  9.1 41.1 all-gather.4
  52.9 60.5 all-gather.6
  129.1 237.2 all-reduce.2
  393.8 33.4 all-gather.8
  429.7 60.5 all-gather.10
  505.8 237.1 all-reduce.4
where the time goes:
time: 778 us; the launch traced here: 777 us
  waiting for transfers between devices  659 us (85%)
  other arithmetic  51.9 us (7%)
  local copies, waits for them, and re-layouts  28.3 us (4%)
  matrix products  23.6 us (3%)
  between operations  13.7 us (2%)
    psum x2, waiting for transfers between devices, per_device(): gram = lax.psum(local_gram, ('grp', 'blk')) / total_rows  471 us
    all_gather x2, waiting for transfers between devices, per_device(): everything = lax.all_gather(local_rows, 'grp', axis=0, tiled=True)  117 us
    all_gather x2, waiting for transfers between devices, per_device(): group_table = lax.all_gather(local_rows, 'blk', axis=0, tiled=True)  70 us
    another operation x6, other arithmetic, per_device(): factor = jnp.linalg.cholesky(gram)  24.8 us
    another operation x4, other arithmetic, per_device(): lax.linalg.triangular_solve(factor, identity_matrix, left_side=True, lowe...  20.9 us
  transfers between devices with their start and end apart: 6, of which 6 were waited for; matrix products, arithmetic and copies ran while one was open for 2% of the time, Pallas kernels for 0%

commit v1 on v0

--- a/solution.py
+++ b/solution.py
@@ -4,6 +4,19 @@
 from jax.sharding import PartitionSpec as P
 
 ITERS = 2
+
+
+def gather_around(shard, axis, dim):
+    ways = lax.axis_size(axis)
+    up = [(d, (d + 1) % ways) for d in range(ways)]
+    down = [(d, (d - 1) % ways) for d in range(ways)]
+    earlier, later = ([shard], [shard])
+    for _ in range(ways // 2):
+        earlier.append(lax.ppermute(earlier[-1], axis, up))
+    for _ in range((ways - 1) // 2):
+        later.append(lax.ppermute(later[-1], axis, down))
+    line = jnp.concatenate([*earlier[::-1], *later[1:]], axis=dim)
+    return jnp.roll(line, (lax.axis_index(axis) - ways // 2) * shard.shape[dim], axis=dim)
 
 
 def per_device(tiles_near, near_cols, tiles_far, far_groups, need_blocks, start_vectors):
@@ -24,7 +37,7 @@
     vectors = start_vectors.astype(jnp.float32)
     for iteration in range(ITERS):
         local_rows = current.reshape(blocks, tile_size, vec_width)
-        group_table = lax.all_gather(local_rows, "blk", axis=0, tiled=True)
+        group_table = gather_around(local_rows, "blk", 0)
         source_ids = jnp.arange(group_size, dtype=jnp.int32)[None, :, None]
         chosen = group_table[source_ids * blocks + near_index]
         near_part = jnp.einsum(

time: 778 us -> 694 us (0.89)
  waiting for transfers between devices: 659 us -> 543 us
  starting transfers between devices: 0.38 us -> 22.6 us
    all_gather x2, waiting for transfers between devices: 117 us -> 32.9 us  [per_device(): everything = lax.all_gather(local_rows, 'grp', axis=0, tiled=True)]
    all_gather x2 -> x0, waiting for transfers between devices: 70 us -> none  [per_device(): group_table = lax.all_gather(local_rows, 'blk', axis=0, tiled=True)]
    ppermute x0 -> x14, waiting for transfers between devices: none -> 38.9 us  [the longest x8 36.9 us: gather_around(): earlier.append(lax.ppermute(earlier[-1], axis, up))]
    ppermute x0 -> x14, starting transfers between devices: none -> 22.3 us  [the longest x6 17.9 us: gather_around(): later.append(lax.ppermute(later[-1], axis, down))]
  transfers between devices with their start and end apart: 6 -> 18, of which waited for: 6 -> 13; matrix products, arithmetic and copies ran while one was open for 2% -> 4% of each run, Pallas kernels for 0% -> 0%
where the time goes in v1:
time: 694 us; the launch traced here: 693 us
  waiting for transfers between devices  543 us (78%)
  other arithmetic  56 us (8%)
  local copies, waits for them, and re-layouts  34.7 us (5%)
  matrix products  23.6 us (3%)
  starting transfers between devices  22.6 us (3%)
  between operations  13.5 us (2%)
    psum x2, waiting for transfers between devices, per_device(): gram = lax.psum(local_gram, ('grp', 'blk')) / total_rows  470 us
    ppermute x8, waiting for transfers between devices, gather_around(): earlier.append(lax.ppermute(earlier[-1], axis, up))  36.9 us
    all_gather x2, waiting for transfers between devices, per_device(): everything = lax.all_gather(local_rows, 'grp', axis=0, tiled=True)  32.9 us
    another operation x6, other arithmetic, per_device(): factor = jnp.linalg.cholesky(gram)  24.8 us
    another operation x4, other arithmetic, per_device(): lax.linalg.triangular_solve(factor, identity_matrix, left_side=True, lowe...  20.9 us
    ppermute x6, starting transfers between devices, gather_around(): later.append(lax.ppermute(later[-1], axis, down))  17.9 us
  transfers between devices with their start and end apart: 18, of which 13 were waited for; matrix products, arithmetic and copies ran while one was open for 4% of the time, Pallas kernels for 0%

profile of v1, /device:TPU:1, one launch (start us, length us, event | category | flops | bytes accessed | tf_op | source)
XLA Modules:
  0.0 693.3 jit_solution(5461220925311783258)
XLA Ops:
  7.3 2.5 collective-permute-start
  9.8 4.0 collective-permute-start.4
  14.5 1.3 reduce.10
  15.8 4.2 collective-permute-done
  20.1 7.8 %collective-permute-done.1 = bf16[4,256,128]{2,1,0:T(8,128)(2,1)} collective-permute-done((bf16[4,256,128]{2,1,0:T(8,128)(2,1)S(1)}, bf16[4,256,128]{2,1,0:T(8,128)(2,1)}, u32[]{:S(2)}, u32[]{:S(2)}) %collective-permute-start.1) | collective-permute-done | bytes 262176 | tf_op jit(solution)/shard_map/ppermute | solution.py:15
  27.9 1.3 reduce.11
  29.2 1.4 gather_fusion.1
  30.9 2.7 collective-permute-start.5
  33.6 1.5 collective-permute-done.2
  35.3 1.9 collective-permute-done.5
  37.2 3.1 collective-permute-start.6
  40.4 1.5 collective-permute-done.3
  42.8 1.0 constant_dynamic-update-slice_fusion.6
  43.8 1.0 constant_dynamic-update-slice_fusion.5
  44.8 1.0 constant_dynamic-update-slice_fusion.4
  45.8 1.0 constant_dynamic-update-slice_fusion.2
  47.9 2.1 fusion.7
  50.0 4.7 gather_fusion
  54.7 17.4 %all-gather.3.cloned.1.call-done = bf16[128,256,128]{2,1,0:T(8,128)(2,1)} async-done(((bf16[4,256,128]{2,1,0:T(8,128)(2,1)}), bf16[128,256,128]{2,1,0:T(8,128)(2,1)}) %all-gather.3.cloned.1.call-update) | async-done | bytes 8388624 | tf_op jit(solution)/shard_map/all_gather | solution.py:46
  72.1 5.3 gather_fusion.2
  77.4 2.7 convolution_bitcast_fusion.1
  80.2 5.2 fusion.33
  86.2 1.2 convolution_bitcast_fusion.3
  87.7 2.0 copy.32
  89.7 235.1 %all-reduce.3.cloned.1.call-done = f32[128,128]{0,1:T(8,128)} async-done(((f32[128,128]{0,1:T(8,128)}), f32[128,128]{0,1:T(8,128)}) %all-reduce.3.cloned.1.call-update) | async-done | bytes 65552 | tf_op jit(solution)/shard_map/psum | solution.py:59
  326.6 11.7 %cholesky.44 = f32[128,128]{1,0:T(8,128)S(1)} custom-call(f32[128,128]{1,0:T(8,128)S(1)} %fusion.47), custom_call_target="Cholesky" | custom-call | tf_op jit(solution)/shard_map/jit(cholesky)/cholesky | solution.py:60
  339.6 9.8 %custom-call.6 = f32[1,128,128]{1,2,0:T(8,128)S(1)} custom-call(f32[1,128,128]{2,1,0:T(8,128)S(1)} %fusion.42), custom_call_target="InvertDiagBlocksLowerTriangular" | custom-call | tf_op jit(solution)/shard_map/triangular_solve/custom-call.0 | solution.py:62
  349.7 2.3 convolution_convert_fusion
  352.1 1.8 collective-permute-start.7
  354.0 7.7 %collective-permute-done.7 = bf16[4,256,128]{2,1,0:T(8,128)(2,1)S(1)} collective-permute-done((bf16[4,256,128]{2,1,0:T(8,128)(2,1)}, bf16[4,256,128]{2,1,0:T(8,128)(2,1)S(1)}, u32[]{:S(2)}, u32[]{:S(2)}) %collective-permute-start.7) | collective-permute-done | bytes 262176 | tf_op jit(solution)/shard_map/ppermute | solution.py:15
  361.7 2.7 collective-permute-start.11
  364.4 5.7 collective-permute-done.8
  370.1 2.7 collective-permute-start.12
  372.8 4.8 collective-permute-done.9
  377.6 2.7 collective-permute-start.13
  380.3 3.8 collective-permute-done.10
  384.4 2.1 fusion.6
  386.5 4.6 gather_fusion.3
  391.1 15.6 %all-gather.5.cloned.1.call-done = bf16[128,256,128]{2,1,0:T(8,128)(2,1)} async-done(((bf16[4,256,128]{2,1,0:T(8,128)(2,1)}), bf16[128,256,128]{2,1,0:T(8,128)(2,1)}) %all-gather.5.cloned.1.call-update) | async-done | bytes 8388624 | tf_op jit(solution)/shard_map/all_gather | solution.py:46
  406.7 5.3 gather_fusion.4
  412.0 2.7 convolution_bitcast_fusion
  414.8 5.2 fusion.23
  420.8 1.2 convolution_bitcast_fusion.2
  422.0 2.0 copy.39
  424.1 235.3 %all-reduce.5.cloned.1.call-done = f32[128,128]{0,1:T(8,128)} async-done(((f32[128,128]{0,1:T(8,128)}), f32[128,128]{0,1:T(8,128)}) %all-reduce.5.cloned.1.call-update) | async-done | bytes 65552 | tf_op jit(solution)/shard_map/psum | solution.py:59
  661.2 11.7 %cholesky.55 = f32[128,128]{1,0:T(8,128)S(1)} custom-call(f32[128,128]{1,0:T(8,128)S(1)} %fusion.45), custom_call_target="Cholesky" | custom-call | tf_op jit(solution)/shard_map/jit(cholesky)/cholesky | solution.py:60
  674.3 9.8 %custom-call.7 = f32[1,128,128]{1,2,0:T(8,128)S(1)} custom-call(f32[1,128,128]{2,1,0:T(8,128)S(1)} %fusion.43), custom_call_target="InvertDiagBlocksLowerTriangular" | custom-call | tf_op jit(solution)/shard_map/triangular_solve/custom-call.0 | solution.py:62
  684.4 2.4 fusion.48
  (75 shorter events, 13.0 us)
Async XLA Ops:
  6.5 70.9 %copy-start = (bf16[24,256,256]{2,1,0:T(8,128)(2,1)S(1)}, bf16[24,256,256]{2,1,0:T(8,128)(2,1)}, u32[]{:S(2)}) copy-start(bf16[24,256,256]{2,1,0:T(8,128)(2,1)} %param.13) | copy-start | bytes 9437188
  6.5 65.5 %all-gather.3.cloned.1.call-start = ((), (), s32[]{:S(2)}) async-start(), calls=%async_computation | async-start | bytes 8650752 | tf_op jit(solution)/shard_map/all_gather | solution.py:46
  7.3 317.5 %all-reduce.3.cloned.1.call-start = ((), (), s32[]{:S(2)}) async-start(), calls=%async_computation.1 | async-start | bytes 131072 | tf_op jit(solution)/shard_map/psum | solution.py:59
  7.3 12.7 %collective-permute-start = (bf16[4,256,128]{2,1,0:T(8,128)(2,1)}, bf16[4,256,128]{2,1,0:T(8,128)(2,1)S(1)}, u32[]{:S(2)}, u32[]{:S(2)}) collective-permute-start(bf16[4,256,128]{2,1,0:T(8,128)(2,1)} %bitcast.93), channel_id=1, source_target_pairs={{0,1},{1,2},{2,3},{3,4},{4,5},{5,6},{6,7},{7,0},{8,9},{9,10},{10,1... | collective-permute-start | bytes 786440 | tf_op jit(solution)/shard_map/ppermute | solution.py:15
  9.8 21.1 %collective-permute-start.4 = (bf16[4,256,128]{2,1,0:T(8,128)(2,1)}, bf16[4,256,128]{2,1,0:T(8,128)(2,1)}, u32[]{:S(2)}, u32[]{:S(2)}) collective-permute-start(bf16[4,256,128]{2,1,0:T(8,128)(2,1)} %bitcast.94), channel_id=1, source_target_pairs={{0,7},{1,0},{2,1},{3,2},{4,3},{5,4},{6,5},{7,6},{8,15},{9,8},{10,9... | collective-permute-start | bytes 786440 | tf_op jit(solution)/shard_map/ppermute | solution.py:17
  20.0 9.2 %copy-start.7 = (bf16[4,256,128]{2,1,0:T(8,128)(2,1)}, bf16[4,256,128]{2,1,0:T(8,128)(2,1)S(1)}, u32[]{:S(2)}) copy-start(bf16[4,256,128]{2,1,0:T(8,128)(2,1)S(1)} %collective-permute-done) | copy-start | bytes 786436
  20.0 7.9 %collective-permute-start.1 = (bf16[4,256,128]{2,1,0:T(8,128)(2,1)S(1)}, bf16[4,256,128]{2,1,0:T(8,128)(2,1)}, u32[]{:S(2)}, u32[]{:S(2)}) collective-permute-start(bf16[4,256,128]{2,1,0:T(8,128)(2,1)S(1)} %collective-permute-done), channel_id=1, source_target_pairs={{0,1},{1,2},{2,3},{3,4},{4,5},{5,6},{6,7},{7,0},{8,9},{9,10},{10,1... | collective-permute-start | bytes 786440 | tf_op jit(solution)/shard_map/ppermute | solution.py:15
  27.9 7.2 %collective-permute-start.2 = (bf16[4,256,128]{2,1,0:T(8,128)(2,1)}, bf16[4,256,128]{2,1,0:T(8,128)(2,1)}, u32[]{:S(2)}, u32[]{:S(2)}) collective-permute-start(bf16[4,256,128]{2,1,0:T(8,128)(2,1)} %collective-permute-done.1), channel_id=1, source_target_pairs={{0,1},{1,2},{2,3},{3,4},{4,5},{5,6},{6,7},{7,0},{8,9},{9,10},{10,1... | collective-permute-start | bytes 786440 | tf_op jit(solution)/shard_map/ppermute | solution.py:15
  29.2 16.6 %copy-start.6 = (bf16[1024,128]{1,0:T(8,128)(2,1)S(1)}, bf16[1024,128]{1,0:T(8,128)(2,1)}, u32[]{:S(2)}) copy-start(bf16[1024,128]{1,0:T(8,128)(2,1)} %param.16) | copy-start | bytes 786436
  30.9 6.3 collective-permute-start.5
  35.1 6.7 collective-permute-start.3
  37.2 10.6 %collective-permute-start.6 = (bf16[4,256,128]{2,1,0:T(8,128)(2,1)}, bf16[4,256,128]{2,1,0:T(8,128)(2,1)S(1)}, u32[]{:S(2)}, u32[]{:S(2)}) collective-permute-start(bf16[4,256,128]{2,1,0:T(8,128)(2,1)} %collective-permute-done.5), channel_id=1, source_target_pairs={{0,7},{1,0},{2,1},{3,2},{4,3},{5,4},{6,5},{7,6},{8,15},{9,8},{10,9... | collective-permute-start | bytes 786440 | tf_op jit(solution)/shard_map/ppermute | solution.py:17
  77.4 2.7 copy-start.4
  85.4 0.8 copy-start.1
  87.4 319.2 %all-gather.5.cloned.1.call-start = ((), (), s32[]{:S(2)}) async-start(), calls=%async_computation.2 | async-start | bytes 8650752 | tf_op jit(solution)/shard_map/all_gather | solution.py:46
  352.1 32.1 %copy-start.5 = (bf16[1024,128]{1,0:T(8,128)(2,1)S(1)}, bf16[1024,128]{1,0:T(8,128)(2,1)}, u32[]{:S(2)}) copy-start(bf16[1024,128]{1,0:T(8,128)(2,1)} %convolution_convert_fusion) | copy-start | bytes 786436
  352.1 307.3 %all-reduce.5.cloned.1.call-start = ((), (), s32[]{:S(2)}) async-start(), calls=%async_computation.3 | async-start | bytes 131072 | tf_op jit(solution)/shard_map/psum | solution.py:59
  352.1 9.6 %collective-permute-start.7 = (bf16[4,256,128]{2,1,0:T(8,128)(2,1)}, bf16[4,256,128]{2,1,0:T(8,128)(2,1)S(1)}, u32[]{:S(2)}, u32[]{:S(2)}) collective-permute-start(bf16[4,256,128]{2,1,0:T(8,128)(2,1)} %bitcast.87), channel_id=1, source_target_pairs={{0,1},{1,2},{2,3},{3,4},{4,5},{5,6},{6,7},{7,0},{8,9},{9,10},{10,1... | collective-permute-start | bytes 786440 | tf_op jit(solution)/shard_map/ppermute | solution.py:15
  361.7 8.4 %collective-permute-start.8 = (bf16[4,256,128]{2,1,0:T(8,128)(2,1)S(1)}, bf16[4,256,128]{2,1,0:T(8,128)(2,1)S(1)}, u32[]{:S(2)}, u32[]{:S(2)}) collective-permute-start(bf16[4,256,128]{2,1,0:T(8,128)(2,1)S(1)} %collective-permute-done.7), channel_id=1, source_target_pairs={{0,1},{1,2},{2,3},{3,4},{4,5},{5,6},{6,7},{7,0},{8,9},{9,10},{10,1... | collective-permute-start | bytes 786440 | tf_op jit(solution)/shard_map/ppermute | solution.py:15
  361.7 8.4 %collective-permute-start.11 = (bf16[4,256,128]{2,1,0:T(8,128)(2,1)}, bf16[4,256,128]{2,1,0:T(8,128)(2,1)S(1)}, u32[]{:S(2)}, u32[]{:S(2)}) collective-permute-start(bf16[4,256,128]{2,1,0:T(8,128)(2,1)} %bitcast.88), channel_id=1, source_target_pairs={{0,7},{1,0},{2,1},{3,2},{4,3},{5,4},{6,5},{7,6},{8,15},{9,8},{10,9... | collective-permute-start | bytes 786440 | tf_op jit(solution)/shard_map/ppermute | solution.py:17
  370.1 7.5 %collective-permute-start.9 = (bf16[4,256,128]{2,1,0:T(8,128)(2,1)S(1)}, bf16[4,256,128]{2,1,0:T(8,128)(2,1)S(1)}, u32[]{:S(2)}, u32[]{:S(2)}) collective-permute-start(bf16[4,256,128]{2,1,0:T(8,128)(2,1)S(1)} %collective-permute-done.8), channel_id=1, source_target_pairs={{0,1},{1,2},{2,3},{3,4},{4,5},{5,6},{6,7},{7,0},{8,9},{9,10},{10,1... | collective-permute-start | bytes 786440 | tf_op jit(solution)/shard_map/ppermute | solution.py:15
  370.1 7.5 %collective-permute-start.12 = (bf16[4,256,128]{2,1,0:T(8,128)(2,1)S(1)}, bf16[4,256,128]{2,1,0:T(8,128)(2,1)S(1)}, u32[]{:S(2)}, u32[]{:S(2)}) collective-permute-start(bf16[4,256,128]{2,1,0:T(8,128)(2,1)S(1)} %collective-permute-done.11), channel_id=1, source_target_pairs={{0,7},{1,0},{2,1},{3,2},{4,3},{5,4},{6,5},{7,6},{8,15},{9,8},{10,9... | collective-permute-start | bytes 786440 | tf_op jit(solution)/shard_map/ppermute | solution.py:17
  377.6 6.4 collective-permute-start.10
  377.6 6.7 collective-permute-start.13
  412.0 2.7 copy-start.3
  420.0 0.8 copy-start.2
Sparse Core Ops, SparseCore 0:
  9.9 62.1 all-gather.2
  87.6 237.1 all-reduce.2
  352.2 54.4 all-gather.4
  422.2 237.2 all-reduce.4
